TPU v7x, 256 devices: a whole 4x4x8 slice. The times are simulated.
256 devices in a mesh: sample: 64 (over z, y, core), rep: 4 (over x).
Axes of the slice: x: 4, y: 4, z: 8, core: 2. Of those that a mesh axis runs over, the one named last changes fastest.
Arguments:
- tokens: bfloat16 [32768, 128], P(('sample', 'rep')), may hold values from -6 to 6
- cache: bfloat16 [32768, 48, 256], P(('sample', 'rep')), may hold values from -144 to 144
- gain: float32 [128], replicated, may hold values from 0.25 to 1.75
- w_query: bfloat16 [128, 128], replicated, may hold values from -0.5 to 0.5
- w_key: bfloat16 [128, 128], replicated, may hold values from -0.5 to 0.5
- w_value: bfloat16 [128, 128], replicated, may hold values from -0.5 to 0.5
- w_out: bfloat16 [128, 128], replicated, may hold values from -0.5 to 0.5
- w_head: bfloat16 [128, 4], replicated, may hold values from -0.5 to 0.5
- coef: float32 [32768], P(('sample', 'rep')), may hold values from -0.625 to 0.625
- chosen: int32 [32768], P(('sample', 'rep')), may hold values from 0 to 3
- dest: int32 [32768, 1], P(('sample', 'rep')), may hold values from 0 to 63; in each aligned block of 128 rows (0 to 127, 128 to 255, ...) at most 4 rows name the same one
Outputs:
- new_cache: bfloat16 [65536, 49, 256], P(('sample', 'rep'))
- log_probs: float32 [65536, 4], P(('sample', 'rep'))
- grad_out: float32 [128, 128], replicated
- grad_head: float32 [128, 4], replicated
Inputs may be any that keep to these rules, and one draw needn't show every extreme that they name: `dest`: within the rows of one device, no value is named by more than 4 rows, a bound that some block reaches.
All inputs are finite; a program needn't handle non-finite values.
Results may differ from a plain program's by a relative error of at most 0.022.
Values may be sent and summed in bfloat16 or wider, within the bound.
No kernel may reach another device: no remote copies, remote signals or barrier semaphores. Data moves between devices by JAX's collectives and lax.ppermute only.
A program may use at most 64 MiB of HBM per device.

v0:
```python
import math
import jax
import jax.numpy as jnp
from jax import lax
from jax.sharding import PartitionSpec as P

HEADS = 4
OUTCOMES = 4


def decode_rows(tokens, cache, coef, chosen, gain, w_query, w_key, w_value, w_out, w_head):
    count = tokens.shape[0]
    width = tokens.shape[1]
    levels = cache.shape[1]
    size = width // HEADS
    xf = tokens.astype(jnp.float32)
    normed = (xf * lax.rsqrt(jnp.mean(xf * xf, -1, keepdims=True) + 1e-05) * gain).astype(
        jnp.bfloat16
    )
    query = (
        jnp.dot(normed, w_query, preferred_element_type=jnp.float32) * (1.0 / math.sqrt(size))
    ).astype(jnp.bfloat16)
    key_new = jnp.dot(normed, w_key, preferred_element_type=jnp.float32).astype(jnp.bfloat16)
    value_new = jnp.dot(normed, w_value, preferred_element_type=jnp.float32).astype(jnp.bfloat16)
    query_heads = query.reshape(count, HEADS, size)
    key_rows = cache[:, :, :width].reshape(count, levels, HEADS, size)
    value_rows = cache[:, :, width:].reshape(count, levels, HEADS, size)
    cached_scores = jnp.einsum(
        "yfn,yjfn->yfj", query_heads, key_rows, preferred_element_type=jnp.float32
    )
    score_self = jnp.sum(
        query_heads.astype(jnp.float32) * key_new.astype(jnp.float32).reshape(count, HEADS, size),
        -1,
    )
    top = jnp.maximum(jnp.max(cached_scores, -1), score_self)
    exp_cache = jnp.exp(cached_scores - top[..., None])
    exp_self = jnp.exp(score_self - top)
    total = jnp.sum(exp_cache, -1) + exp_self
    cached_weights = (exp_cache / total[..., None]).astype(jnp.bfloat16)
    weight_self = (exp_self / total).astype(jnp.bfloat16)
    attention_output = jnp.einsum(
        "jat,jtaf->jaf", cached_weights, value_rows, preferred_element_type=jnp.float32
    )
    attention_output = attention_output + weight_self.astype(jnp.float32)[
        ..., None
    ] * value_new.astype(jnp.float32).reshape(count, HEADS, size)
    attention_output = attention_output.reshape(count, width).astype(jnp.bfloat16)
    hidden = (xf + jnp.dot(attention_output, w_out, preferred_element_type=jnp.float32)).astype(
        jnp.bfloat16
    )
    logits = jnp.dot(hidden, w_head, preferred_element_type=jnp.float32)
    logp = jax.nn.log_softmax(logits, -1)
    picked = (chosen[:, None] == jnp.arange(OUTCOMES, dtype=jnp.int32)[None, :]).astype(jnp.float32)
    dlog = coef[:, None] * (picked - jnp.exp(logp))
    grad_head = jnp.dot(hidden.astype(jnp.float32).T, dlog, precision=lax.Precision.HIGHEST)
    hidden_gradient = jnp.dot(dlog, w_head.astype(jnp.float32).T, precision=lax.Precision.HIGHEST)
    grad_out = jnp.dot(
        attention_output.astype(jnp.float32).T, hidden_gradient, precision=lax.Precision.HIGHEST
    )
    both = jnp.concatenate([key_new, value_new], -1)
    return (both, logp, grad_out, grad_head)


def placed(value_rows, place, slots):
    return jnp.zeros((slots,) + value_rows.shape[1:], value_rows.dtype).at[place].set(value_rows)


def on_device(tokens, cache, gain, w_query, w_key, w_value, w_out, w_head, coef, chosen, dest):
    count = tokens.shape[0]
    peers = lax.axis_size("sample")
    capacity = 2 * count // peers
    slots = peers * capacity
    target = dest[:, 0]
    onehot = (target[:, None] == jnp.arange(peers, dtype=jnp.int32)[None, :]).astype(jnp.int32)
    rank = jnp.sum(jnp.cumsum(onehot, 0) * onehot, 1) - 1
    place = target * capacity + rank
    filled = jnp.ones((count,), jnp.int32)
    got_tokens, got_cache, got_coef, got_chosen, got_filled = (
        lax.all_to_all(
            placed(tokens, place, slots), "sample", split_axis=0, concat_axis=0, tiled=True
        ),
        lax.all_to_all(
            placed(cache, place, slots), "sample", split_axis=0, concat_axis=0, tiled=True
        ),
        lax.all_to_all(
            placed(coef, place, slots).astype(jnp.bfloat16),
            "sample",
            split_axis=0,
            concat_axis=0,
            tiled=True,
        ).astype(jnp.float32),
        lax.all_to_all(
            placed(chosen, place, slots), "sample", split_axis=0, concat_axis=0, tiled=True
        ),
        lax.all_to_all(
            placed(filled, place, slots), "sample", split_axis=0, concat_axis=0, tiled=True
        ),
    )
    both, logp, grad_out, grad_head = decode_rows(
        got_tokens, got_cache, got_coef, got_chosen, gain, w_query, w_key, w_value, w_out, w_head
    )
    logp = logp * got_filled[:, None].astype(jnp.float32)
    new_cache = jnp.concatenate([got_cache, both[:, None, :]], 1)
    grad_out, grad_head = lax.psum((grad_out, grad_head), ("sample", "rep"))
    return (new_cache, logp, grad_out, grad_head)


def solution(mesh):
    placed = (
        P(("sample", "rep"), None),
        P(("sample", "rep"), None, None),
        P(),
        P(),
        P(),
        P(),
        P(),
        P(),
        P(("sample", "rep")),
        P(("sample", "rep")),
        P(("sample", "rep"), None),
    )
    return jax.shard_map(
        on_device,
        mesh=mesh,
        in_specs=placed,
        out_specs=(P(("sample", "rep"), None, None), P(("sample", "rep"), None), P(), P()),
        check_vma=False,
    )
```

profile of v0, /device:TPU:1, one launch (start us, length us, event | category | flops | bytes accessed | tf_op | source)
XLA Modules:
  0.0 504.9 jit_solution(15651331253304061399)
XLA Ops:
  7.2 0.9 fusion.8
  8.1 0.2 reduce_window_sum.11
  8.3 0.8 select_reduce_fusion
  9.1 0.7 fusion.13
  9.8 1.1 scatter_custom_fusion.3
  10.9 0.7 all_to_all.36
  11.6 13.2 %all-to-all-start.3 = ((bf16[64,4,1]{1,2,0:T(2,128)(2,1)}), bf16[64,4,1]{1,2,0:T(2,128)(2,1)S(1)}, u32[]{:S(2)}, u32[]{:S(2)}) async-start(bf16[64,4,1]{1,2,0:T(2,128)(2,1)} %all_to_all.36), calls=%async_computation.3 | async-start | bytes 65536 | tf_op jit(solution)/shard_map/all_to_all | solution.py:85
  24.8 1.1 scatter_custom_fusion.4
  25.9 0.7 all_to_all.34
  26.6 7.5 %all-to-all-done.3 = bf16[64,4,1]{1,2,0:T(2,128)(2,1)S(1)} async-done(((bf16[64,4,1]{1,2,0:T(2,128)(2,1)}), bf16[64,4,1]{1,2,0:T(2,128)(2,1)S(1)}, u32[]{:S(2)}, u32[]{:S(2)}) %all-to-all-start.3) | async-done | bytes 544 | tf_op jit(solution)/shard_map/all_to_all | solution.py:85
  34.1 4.7 all-to-all-start.4
  38.8 1.0 scatter_custom_fusion.2
  39.8 0.7 all_to_all.30
  40.5 7.7 %all-to-all-done.4 = s32[64,4,1]{1,2,0:T(1,128)S(1)} async-done(((s32[64,4,1]{1,2,0:T(1,128)}), s32[64,4,1]{1,2,0:T(1,128)S(1)}, u32[]{:S(2)}, u32[]{:S(2)}) %all-to-all-start.4) | async-done | bytes 1056 | tf_op jit(solution)/shard_map/all_to_all | solution.py:92
  48.2 4.7 all-to-all-start.2
  52.9 1.7 scatter_custom_fusion.1
  54.6 7.7 %all-to-all-done.2 = s32[64,4,1]{1,2,0:T(1,128)S(1)} async-done(((s32[64,4,1]{1,2,0:T(1,128)}), s32[64,4,1]{1,2,0:T(1,128)S(1)}, u32[]{:S(2)}, u32[]{:S(2)}) %all-to-all-start.2) | async-done | bytes 1056 | tf_op jit(solution)/shard_map/all_to_all | solution.py:95
  62.3 4.7 all-to-all-start.1
  67.1 3.1 broadcast_in_dim.10
  70.2 16.2 %scatter_fusion = bf16[256,48,256]{2,1,0:T(8,128)(2,1)} fusion(bf16[256,48,256]{2,1,0:T(8,128)(2,1)} %broadcast_in_dim.10, s32[128]{0:T(128)S(1)} %fusion.13, bf16[128,48,256]{2,1,0:T(8,128)(2,1)S(1)} %copy-done.1), kind=kCustom, calls=%fused_computation | custom fusion | bytes 9437696 | tf_op jit(solution)/shard_map/scatter | solution.py:65
  86.4 10.7 %all-to-all-start = ((bf16[256,48,256]{2,1,0:T(8,128)(2,1)}), bf16[256,48,256]{2,1,0:T(8,128)(2,1)}, u32[]{:S(2)}, u32[]{:S(2)}) async-start(bf16[256,48,256]{2,1,0:T(8,128)(2,1)} %scatter_fusion), calls=%async_computation | async-start | bytes 12582912 | tf_op jit(solution)/shard_map/all_to_all | solution.py:82
  97.1 0.2 all-reduce.2.cloned.1.call-start
  97.5 0.5 broadcast.74
  98.0 0.7 reduce.16
  99.0 0.7 convert_element_type.101
  99.9 0.7 multiply_convert_fusion
  100.6 0.2 convolution_convert_fusion.1
  100.8 0.2 convolution_convert_fusion
  101.1 0.9 copy.34
  101.9 0.9 bitcast_convert_fusion
  102.8 132.8 %all-to-all-done = bf16[256,48,256]{2,1,0:T(8,128)(2,1)} async-done(((bf16[256,48,256]{2,1,0:T(8,128)(2,1)}), bf16[256,48,256]{2,1,0:T(8,128)(2,1)}, u32[]{:S(2)}, u32[]{:S(2)}) %all-to-all-start) | async-done | bytes 6291488 | tf_op jit(solution)/shard_map/all_to_all | solution.py:82
  235.6 6.7 %fusion.22 = (bf16[256,48,128]{2,1,0:T(8,128)(2,1)}, bf16[256,48,128]{2,1,0:T(8,128)(2,1)}) fusion(bf16[256,48,256]{2,1,0:T(8,128)(2,1)} %all-to-all-done), kind=kLoop, calls=%fused_computation.55 | loop fusion | bytes 12582912 | tf_op jit(solution)/shard_map/slice | solution.py:26
  242.3 3.9 copy.54
  246.2 2.3 multiply_reduce_fusion.1
  248.7 0.8 copy.58
  249.5 3.9 copy.55
  253.4 1.7 multiply_reduce_fusion
  255.1 1.1 fusion.1
  256.2 0.8 fusion.23
  257.1 0.1 fusion.20
  257.3 1.0 fusion.21
  258.3 0.8 fusion.24
  259.1 3.5 pad_maximum_fusion
  262.7 0.6 subtract_multiply_fusion.1
  263.3 4.3 copy.40
  267.6 78.6 %psum.15 = f32[128,4]{0,1:T(4,128)} all-reduce(f32[128,4]{0,1:T(4,128)S(1)} %fusion.20), channel_id=1, replica_groups=mesh['sample'=64,'rep'=4] {'sample','rep'}, use_global_device_ids=true, to_apply=%region_14.15 | all-reduce | flops 512 | bytes 4096 | tf_op jit(solution)/shard_map/psum | solution.py:104
  346.1 150.5 %all-reduce.2.cloned.1.call-done = f32[128,128]{1,0:T(8,128)} async-done(((f32[128,128]{1,0:T(8,128)}), f32[128,128]{1,0:T(8,128)}) %all-reduce.2.cloned.1.call-update) | async-done | bytes 65552 | tf_op jit(solution)/shard_map/psum | solution.py:104
  496.6 1.5 copy.71
  (37 shorter events, 1.0 us)
Async XLA Ops:
  7.2 94.8 %copy-start = (bf16[128,128]{1,0:T(8,128)(2,1)S(1)}, bf16[128,128]{1,0:T(8,128)(2,1)}, u32[]{:S(2)}) copy-start(bf16[128,128]{1,0:T(8,128)(2,1)} %param.14) | copy-start | bytes 98308
  7.2 63.0 %copy-start.1 = (bf16[128,48,256]{2,1,0:T(8,128)(2,1)S(1)}, bf16[128,48,256]{2,1,0:T(8,128)(2,1)}, u32[]{:S(2)}) copy-start(bf16[128,48,256]{2,1,0:T(8,128)(2,1)} %param.12) | copy-start | bytes 9437188
  11.6 22.5 %all-to-all-start.3 = ((bf16[64,4,1]{1,2,0:T(2,128)(2,1)}), bf16[64,4,1]{1,2,0:T(2,128)(2,1)S(1)}, u32[]{:S(2)}, u32[]{:S(2)}) async-start(bf16[64,4,1]{1,2,0:T(2,128)(2,1)} %all_to_all.36), calls=%async_computation.3 | async-start | bytes 65536 | tf_op jit(solution)/shard_map/all_to_all | solution.py:85
  34.1 14.1 %all-to-all-start.4 = ((s32[64,4,1]{1,2,0:T(1,128)}), s32[64,4,1]{1,2,0:T(1,128)S(1)}, u32[]{:S(2)}, u32[]{:S(2)}) async-start(s32[64,4,1]{1,2,0:T(1,128)} %bitcast.19), calls=%async_computation.4 | async-start | bytes 65536 | tf_op jit(solution)/shard_map/all_to_all | solution.py:92
  48.2 14.1 %all-to-all-start.2 = ((s32[64,4,1]{1,2,0:T(1,128)}), s32[64,4,1]{1,2,0:T(1,128)S(1)}, u32[]{:S(2)}, u32[]{:S(2)}) async-start(s32[64,4,1]{1,2,0:T(1,128)} %bitcast.18), calls=%async_computation.2 | async-start | bytes 65536 | tf_op jit(solution)/shard_map/all_to_all | solution.py:95
  62.3 24.0 %all-to-all-start.1 = ((bf16[64,4,128]{2,1,0:T(4,128)(2,1)}), bf16[64,4,128]{2,1,0:T(4,128)(2,1)S(1)}, u32[]{:S(2)}, u32[]{:S(2)}) async-start(bf16[64,4,128]{2,1,0:T(4,128)(2,1)} %bitcast.5), calls=%async_computation.1 | async-start | bytes 131072 | tf_op jit(solution)/shard_map/all_to_all | solution.py:79
  86.4 13.6 %copy-start.7 = (f32[128]{0:T(128)S(1)}, f32[128]{0:T(128)}, u32[]{:S(2)}) copy-start(f32[128]{0:T(128)} %param.13) | copy-start | bytes 1540
  86.4 14.2 %copy-start.3 = (bf16[128,128]{1,0:T(8,128)(2,1)S(1)}, bf16[128,128]{1,0:T(8,128)(2,1)}, u32[]{:S(2)}) copy-start(bf16[128,128]{1,0:T(8,128)(2,1)} %param.15) | copy-start | bytes 98308
  86.4 14.5 %copy-start.4 = (bf16[128,128]{1,0:T(8,128)(2,1)S(1)}, bf16[128,128]{1,0:T(8,128)(2,1)}, u32[]{:S(2)}) copy-start(bf16[128,128]{1,0:T(8,128)(2,1)} %param.16) | copy-start | bytes 98308
  86.4 149.3 %all-to-all-start = ((bf16[256,48,256]{2,1,0:T(8,128)(2,1)}), bf16[256,48,256]{2,1,0:T(8,128)(2,1)}, u32[]{:S(2)}, u32[]{:S(2)}) async-start(bf16[256,48,256]{2,1,0:T(8,128)(2,1)} %scatter_fusion), calls=%async_computation | async-start | bytes 12582912 | tf_op jit(solution)/shard_map/all_to_all | solution.py:82
  97.1 399.5 %all-reduce.2.cloned.1.call-start = ((), (), s32[]{:S(2)}) async-start(), calls=%async_computation.5 | async-start | bytes 131072 | tf_op jit(solution)/shard_map/psum | solution.py:104
  248.4 6.7 %copy-start.5 = (bf16[128,128]{1,0:T(8,128)(2,1)S(1)}, bf16[128,128]{1,0:T(8,128)(2,1)}, u32[]{:S(2)}) copy-start(bf16[128,128]{1,0:T(8,128)(2,1)} %param.17) | copy-start | bytes 98308
  248.4 10.7 %copy-start.2 = (bf16[256,1,256]{2,1,0:T(2,128)(2,1)S(1)}, bf16[256,1,256]{2,1,0:T(2,128)(2,1)}, u32[]{:S(2)}) copy-start(bf16[256,1,256]{2,1,0:T(2,128)(2,1)} %copy.34) | copy-start | bytes 393220
  259.1 3.5 copy-start.6
Sparse Core Ops, SparseCore 0:
  259.2 237.2 all-reduce.1
where the time goes:
time: 506 us; the launch traced here: 505 us
  waiting for transfers between devices  306 us (60%)
  blocking collectives  78.6 us (16%)
  local copies, waits for them, and re-layouts  49.7 us (10%)
  starting transfers between devices  38.2 us (8%)
  between operations  14.4 us (3%)
  other arithmetic  12.7 us (3%)
  matrix products  5.2 us (1%)
    psum x1, waiting for transfers between devices, on_device(): grad_out, grad_head = lax.psum((grad_out, grad_head), ('sample', 'rep'))  150 us
    all_to_all x1, waiting for transfers between devices, on_device(): lax.all_to_all(placed(cache, place, slots), 'sample', split_axis=0, conca...  133 us
    psum x1, blocking collectives, on_device(): grad_out, grad_head = lax.psum((grad_out, grad_head), ('sample', 'rep'))  78.6 us
    scatter x5, local copies, waits for them, and re-layouts, placed(): jnp.zeros((slots,) + value_rows.shape[1:], value_rows.dtype).at[place]  21.1 us
    unnamed x21, local copies, waits for them, and re-layouts  14.4 us
    all_to_all x1, starting transfers between devices, on_device(): lax.all_to_all(placed(coef, place, slots).astype(jnp.bfloat16), 'sample',...  13.2 us
    all_to_all x1, starting transfers between devices, on_device(): lax.all_to_all(placed(cache, place, slots), 'sample', split_axis=0, conca...  10.7 us
  transfers between devices with their start and end apart: 6, of which 5 were waited for; matrix products, arithmetic and copies ran while one was open for 7% of the time, Pallas kernels for 0%

commit v1 on v0

--- a/solution.py
+++ b/solution.py
@@ -1,3 +1,4 @@
+import functools
 import math
 import jax
 import jax.numpy as jnp
@@ -6,6 +7,15 @@
 
 HEADS = 4
 OUTCOMES = 4
+
+
+def replace_pieces_all(content, chip_axis, along_axis):
+    for i0 in (chip_axis, along_axis):
+        content = lax.psum(content, i0)
+    return content
+
+
+end_vector = functools.partial(replace_pieces_all, chip_axis="rep", along_axis="sample")
 
 
 def decode_rows(tokens, cache, coef, chosen, gain, w_query, w_key, w_value, w_out, w_head):
@@ -101,7 +111,7 @@
     )
     logp = logp * got_filled[:, None].astype(jnp.float32)
     new_cache = jnp.concatenate([got_cache, both[:, None, :]], 1)
-    grad_out, grad_head = lax.psum((grad_out, grad_head), ("sample", "rep"))
+    grad_out, grad_head = end_vector((grad_out, grad_head))
     return (new_cache, logp, grad_out, grad_head)
 
 

time: 506 us -> 483 us (0.955)
  waiting for transfers between devices: 306 us -> 222 us
  blocking collectives: 78.6 us -> 136 us
    psum x1 -> x2, waiting for transfers between devices: 150 us -> 66 us  [replace_pieces_all(): content = lax.psum(content, i0)]
    psum x1 -> x2, blocking collectives: 78.6 us -> 136 us  [replace_pieces_all(): content = lax.psum(content, i0)]
    unnamed x21 -> x19, local copies, waits for them, and re-layouts: 14.4 us -> 16.8 us
  transfers between devices with their start and end apart: 6 -> 7, of which waited for: 5 -> 6; matrix products, arithmetic and copies ran while one was open for 7% -> 9% of each run, Pallas kernels for 0% -> 0%
where the time goes in v1:
time: 483 us; the launch traced here: 482 us
  waiting for transfers between devices  222 us (46%)
  blocking collectives  136 us (28%)
  local copies, waits for them, and re-layouts  51.6 us (11%)
  starting transfers between devices  38.3 us (8%)
  other arithmetic  14.9 us (3%)
  between operations  14.4 us (3%)
    psum x2, blocking collectives, replace_pieces_all(): content = lax.psum(content, i0)  136 us
    all_to_all x1, waiting for transfers between devices, on_device(): lax.all_to_all(placed(cache, place, slots), 'sample', split_axis=0, conca...  133 us
    psum x2, waiting for transfers between devices, replace_pieces_all(): content = lax.psum(content, i0)  66 us
    scatter x5, local copies, waits for them, and re-layouts, placed(): jnp.zeros((slots,) + value_rows.shape[1:], value_rows.dtype).at[place]  21.1 us
    unnamed x19, local copies, waits for them, and re-layouts  16.8 us
    all_to_all x1, starting transfers between devices, on_device(): lax.all_to_all(placed(coef, place, slots).astype(jnp.bfloat16), 'sample',...  13.2 us
    all_to_all x1, starting transfers between devices, on_device(): lax.all_to_all(placed(cache, place, slots), 'sample', split_axis=0, conca...  10.7 us
  transfers between devices with their start and end apart: 7, of which 6 were waited for; matrix products, arithmetic and copies ran while one was open for 9% of the time, Pallas kernels for 0%

profile of v1, /device:TPU:1, one launch (start us, length us, event | category | flops | bytes accessed | tf_op | source)
XLA Modules:
  0.0 481.6 jit_solution(409296845481508)
XLA Ops:
  7.2 0.9 fusion.8
  8.1 0.2 reduce_window_sum.11
  8.3 0.8 select_reduce_fusion
  9.1 0.7 fusion.13
  9.8 1.1 scatter_custom_fusion.3
  10.9 0.7 all_to_all.36
  11.6 13.2 %all-to-all-start.3 = ((bf16[64,4,1]{1,2,0:T(2,128)(2,1)}), bf16[64,4,1]{1,2,0:T(2,128)(2,1)S(1)}, u32[]{:S(2)}, u32[]{:S(2)}) async-start(bf16[64,4,1]{1,2,0:T(2,128)(2,1)} %all_to_all.36), calls=%async_computation.3 | async-start | bytes 65536 | tf_op jit(solution)/shard_map/all_to_all | solution.py:95
  24.8 1.1 scatter_custom_fusion.4
  25.9 0.7 all_to_all.34
  26.6 7.5 %all-to-all-done.3 = bf16[64,4,1]{1,2,0:T(2,128)(2,1)S(1)} async-done(((bf16[64,4,1]{1,2,0:T(2,128)(2,1)}), bf16[64,4,1]{1,2,0:T(2,128)(2,1)S(1)}, u32[]{:S(2)}, u32[]{:S(2)}) %all-to-all-start.3) | async-done | bytes 544 | tf_op jit(solution)/shard_map/all_to_all | solution.py:95
  34.1 4.7 all-to-all-start.4
  38.8 1.0 scatter_custom_fusion.2
  39.8 0.7 all_to_all.30
  40.5 7.7 %all-to-all-done.4 = s32[64,4,1]{1,2,0:T(1,128)S(1)} async-done(((s32[64,4,1]{1,2,0:T(1,128)}), s32[64,4,1]{1,2,0:T(1,128)S(1)}, u32[]{:S(2)}, u32[]{:S(2)}) %all-to-all-start.4) | async-done | bytes 1056 | tf_op jit(solution)/shard_map/all_to_all | solution.py:102
  48.2 4.7 all-to-all-start.2
  52.9 1.7 scatter_custom_fusion.1
  54.6 7.7 %all-to-all-done.2 = s32[64,4,1]{1,2,0:T(1,128)S(1)} async-done(((s32[64,4,1]{1,2,0:T(1,128)}), s32[64,4,1]{1,2,0:T(1,128)S(1)}, u32[]{:S(2)}, u32[]{:S(2)}) %all-to-all-start.2) | async-done | bytes 1056 | tf_op jit(solution)/shard_map/all_to_all | solution.py:105
  62.3 4.7 all-to-all-start.1
  67.1 3.1 broadcast_in_dim.10
  70.2 16.2 %scatter_fusion = bf16[256,48,256]{2,1,0:T(8,128)(2,1)} fusion(bf16[256,48,256]{2,1,0:T(8,128)(2,1)} %broadcast_in_dim.10, s32[128]{0:T(128)S(1)} %fusion.13, bf16[128,48,256]{2,1,0:T(8,128)(2,1)S(1)} %copy-done.1), kind=kCustom, calls=%fused_computation | custom fusion | bytes 9437696 | tf_op jit(solution)/shard_map/scatter | solution.py:75
  86.4 10.7 %all-to-all-start = ((bf16[256,48,256]{2,1,0:T(8,128)(2,1)}), bf16[256,48,256]{2,1,0:T(8,128)(2,1)}, u32[]{:S(2)}, u32[]{:S(2)}) async-start(bf16[256,48,256]{2,1,0:T(8,128)(2,1)} %scatter_fusion), calls=%async_computation | async-start | bytes 12582912 | tf_op jit(solution)/shard_map/all_to_all | solution.py:92
  97.1 0.2 all-reduce.3.cloned.1.call-start
  97.5 0.5 broadcast.74
  98.0 0.7 reduce.16
  99.1 0.1 multiply_reduce_fusion.2
  99.4 0.7 multiply_convert_fusion
  100.0 0.2 convolution_convert_fusion.1
  100.3 0.2 convolution_convert_fusion
  100.5 0.9 copy.34
  101.4 0.9 bitcast_convert_fusion
  102.2 133.4 %all-to-all-done = bf16[256,48,256]{2,1,0:T(8,128)(2,1)} async-done(((bf16[256,48,256]{2,1,0:T(8,128)(2,1)}), bf16[256,48,256]{2,1,0:T(8,128)(2,1)}, u32[]{:S(2)}, u32[]{:S(2)}) %all-to-all-start) | async-done | bytes 6291488 | tf_op jit(solution)/shard_map/all_to_all | solution.py:92
  235.6 6.6 %fusion.22 = (bf16[256,48,128]{2,1,0:T(8,128)(2,1)}, bf16[256,48,128]{2,1,0:T(8,128)(2,1)}) fusion(bf16[256,48,256]{2,1,0:T(8,128)(2,1)} %all-to-all-done), kind=kLoop, calls=%fused_computation.55 | loop fusion | bytes 12582912 | tf_op jit(solution)/shard_map/slice | solution.py:36
  242.2 3.9 copy.54
  246.1 2.3 multiply_reduce_fusion.1
  248.8 3.9 copy.55
  252.7 0.9 multiply_reduce_fusion
  253.6 1.1 fusion.1
  254.7 0.2 fusion.23
  254.9 0.3 fusion.21
  255.3 0.8 fusion.24
  256.2 6.6 %pad_maximum_fusion = bf16[256,49,256]{2,1,0:T(8,128)(2,1)} fusion(bf16[256,1,256]{2,1,0:T(2,128)(2,1)} %copy.34, bf16[256,48,256]{2,1,0:T(8,128)(2,1)} %all-to-all-done), kind=kLoop, calls=%fused_computation.5 | loop fusion | flops 12845056 | bytes 12845056 | tf_op jit(solution)/shard_map/concatenate | solution.py:113
  262.9 36.2 %all-reduce.3.cloned.1.call-done = f32[128,128]{1,0:T(8,128)} async-done(((f32[128,128]{1,0:T(8,128)}), f32[128,128]{1,0:T(8,128)}) %all-reduce.3.cloned.1.call-update) | async-done | bytes 65552 | tf_op jit(solution)/shard_map/psum | solution.py:14
  299.2 0.6 subtract_multiply_fusion.1
  299.8 7.4 %copy.40 = bf16[256,49,256]{2,0,1:T(8,128)(2,1)} copy(bf16[256,49,256]{2,1,0:T(8,128)(2,1)} %pad_maximum_fusion) | data formatting | bytes 12845056
  307.1 7.4 %psum.30 = f32[128,4]{0,1:T(4,128)S(1)} all-reduce(f32[128,4]{0,1:T(4,128)S(1)} %fusion.20), channel_id=1, replica_groups=mesh['sample'=64,'rep'=4] {'rep'}, use_global_device_ids=true, to_apply=%region_15.16 | all-reduce | flops 512 | bytes 4096 | tf_op jit(solution)/shard_map/psum | solution.py:14
  314.5 129.0 %psum.31 = f32[128,4]{0,1:T(4,128)} all-reduce(f32[128,4]{0,1:T(4,128)S(1)} %psum.30), channel_id=1, replica_groups=mesh['sample'=64,'rep'=4] {'sample'}, use_global_device_ids=true, to_apply=%region_16.17 | all-reduce | flops 512 | bytes 4096 | tf_op jit(solution)/shard_map/psum | solution.py:14
  443.5 29.7 %all-reduce.5.cloned.1.call-done = f32[128,128]{1,0:T(8,128)} async-done(((f32[128,128]{1,0:T(8,128)}), f32[128,128]{1,0:T(8,128)}) %all-reduce.5.cloned.1.call-update) | async-done | bytes 65552 | tf_op jit(solution)/shard_map/psum | solution.py:14
  473.3 1.5 copy.72
  (39 shorter events, 1.3 us)
Async XLA Ops:
  7.2 94.2 %copy-start = (bf16[128,128]{1,0:T(8,128)(2,1)S(1)}, bf16[128,128]{1,0:T(8,128)(2,1)}, u32[]{:S(2)}) copy-start(bf16[128,128]{1,0:T(8,128)(2,1)} %param.14) | copy-start | bytes 98308
  7.2 63.0 %copy-start.1 = (bf16[128,48,256]{2,1,0:T(8,128)(2,1)S(1)}, bf16[128,48,256]{2,1,0:T(8,128)(2,1)}, u32[]{:S(2)}) copy-start(bf16[128,48,256]{2,1,0:T(8,128)(2,1)} %param.12) | copy-start | bytes 9437188
  11.6 22.5 %all-to-all-start.3 = ((bf16[64,4,1]{1,2,0:T(2,128)(2,1)}), bf16[64,4,1]{1,2,0:T(2,128)(2,1)S(1)}, u32[]{:S(2)}, u32[]{:S(2)}) async-start(bf16[64,4,1]{1,2,0:T(2,128)(2,1)} %all_to_all.36), calls=%async_computation.3 | async-start | bytes 65536 | tf_op jit(solution)/shard_map/all_to_all | solution.py:95
  34.1 14.1 %all-to-all-start.4 = ((s32[64,4,1]{1,2,0:T(1,128)}), s32[64,4,1]{1,2,0:T(1,128)S(1)}, u32[]{:S(2)}, u32[]{:S(2)}) async-start(s32[64,4,1]{1,2,0:T(1,128)} %bitcast.19), calls=%async_computation.4 | async-start | bytes 65536 | tf_op jit(solution)/shard_map/all_to_all | solution.py:102
  48.2 14.1 %all-to-all-start.2 = ((s32[64,4,1]{1,2,0:T(1,128)}), s32[64,4,1]{1,2,0:T(1,128)S(1)}, u32[]{:S(2)}, u32[]{:S(2)}) async-start(s32[64,4,1]{1,2,0:T(1,128)} %bitcast.18), calls=%async_computation.2 | async-start | bytes 65536 | tf_op jit(solution)/shard_map/all_to_all | solution.py:105
  62.3 24.0 %all-to-all-start.1 = ((bf16[64,4,128]{2,1,0:T(4,128)(2,1)}), bf16[64,4,128]{2,1,0:T(4,128)(2,1)S(1)}, u32[]{:S(2)}, u32[]{:S(2)}) async-start(bf16[64,4,128]{2,1,0:T(4,128)(2,1)} %bitcast.5), calls=%async_computation.1 | async-start | bytes 131072 | tf_op jit(solution)/shard_map/all_to_all | solution.py:89
  86.4 13.0 %copy-start.6 = (f32[128]{0:T(128)S(1)}, f32[128]{0:T(128)}, u32[]{:S(2)}) copy-start(f32[128]{0:T(128)} %param.13) | copy-start | bytes 1540
  86.4 13.7 %copy-start.2 = (bf16[128,128]{1,0:T(8,128)(2,1)S(1)}, bf16[128,128]{1,0:T(8,128)(2,1)}, u32[]{:S(2)}) copy-start(bf16[128,128]{1,0:T(8,128)(2,1)} %param.15) | copy-start | bytes 98308
  86.4 13.9 %copy-start.3 = (bf16[128,128]{1,0:T(8,128)(2,1)S(1)}, bf16[128,128]{1,0:T(8,128)(2,1)}, u32[]{:S(2)}) copy-start(bf16[128,128]{1,0:T(8,128)(2,1)} %param.16) | copy-start | bytes 98308
  86.4 149.3 %all-to-all-start = ((bf16[256,48,256]{2,1,0:T(8,128)(2,1)}), bf16[256,48,256]{2,1,0:T(8,128)(2,1)}, u32[]{:S(2)}, u32[]{:S(2)}) async-start(bf16[256,48,256]{2,1,0:T(8,128)(2,1)} %scatter_fusion), calls=%async_computation | async-start | bytes 12582912 | tf_op jit(solution)/shard_map/all_to_all | solution.py:92
  97.1 202.0 %all-reduce.3.cloned.1.call-start = ((), (), s32[]{:S(2)}) async-start(), calls=%async_computation.5 | async-start | bytes 131072 | tf_op jit(solution)/shard_map/psum | solution.py:14
  248.4 5.2 %copy-start.4 = (bf16[128,128]{1,0:T(8,128)(2,1)S(1)}, bf16[128,128]{1,0:T(8,128)(2,1)}, u32[]{:S(2)}) copy-start(bf16[128,128]{1,0:T(8,128)(2,1)} %param.17) | copy-start | bytes 98308
  248.4 6.3 %copy-start.5 = (bf16[128,4]{0,1:T(4,128)(2,1)S(1)}, bf16[128,4]{0,1:T(4,128)(2,1)}, u32[]{:S(2)}) copy-start(bf16[128,4]{0,1:T(4,128)(2,1)} %param.18) | copy-start | bytes 3076
  256.1 217.1 %all-reduce.5.cloned.1.call-start = ((), (), s32[]{:S(2)}) async-start(), calls=%async_computation.6 | async-start | bytes 131072 | tf_op jit(solution)/shard_map/psum | solution.py:14
Sparse Core Ops, SparseCore 0:
  256.2 42.8 all-reduce.2
  303.0 170.2 all-reduce.4
